TPU v7x, 32 devices: a whole 2x2x4 slice. The times are simulated.
32 devices in a mesh: groups: 2 (over y), seq: 16 (over z, x, core).
Axes of the slice: x: 2, y: 2, z: 4, core: 2. Of those that a mesh axis runs over, the one named last changes fastest.
Arguments:
- hidden: bfloat16 [4, 4, 8192], P('groups', None, 'seq'), parts along dimension 0, may hold values from -1200 to 1200
- norm_gain: bfloat16 [8192], P('seq'), may hold values from 0.099609375 to 1.8984375
- q_weight: bfloat16 [8192, 8192], P('seq'), may hold values from -0.0625 to 0.0625
- kv_weight: bfloat16 [8192, 2048], P('seq'), may hold values from -0.0625 to 0.0625
- out_weight: bfloat16 [8192, 8192], P('seq'), may hold values from -0.09375 to 0.09375
- head_kind: int32 [8], replicated, may hold values from 0 to 1, as said below
- ret_keys: bfloat16 [4, 4, 32768, 128], P('groups', None, 'seq'), parts along dimension 0, may hold values from -600 to 600
- ret_values: bfloat16 [4, 4, 32768, 128], P('groups', None, 'seq'), parts along dimension 0, may hold values from -8 to 8
- stream_keys: bfloat16 [4, 4, 2048, 128], P('groups', None, 'seq'), parts along dimension 0, may hold values from -600 to 600
- stream_values: bfloat16 [4, 4, 2048, 128], P('groups', None, 'seq'), parts along dimension 0, may hold values from -8 to 8
- cache_len: int32 [4], P('groups'), parts along dimension 0, may hold values from 1 to 32768, as said below
- sink_len: int32 [4], P('groups'), parts along dimension 0, may hold values from 1 to 128, as said below
- window_len: int32 [4], P('groups'), parts along dimension 0, may hold values from 1 to 1920, as said below
Outputs:
- layer_output: bfloat16 [4, 4, 8192], P('groups', None, 'seq'), parts along dimension 0
- new_entries: bfloat16 [4, 4, 2048], P('groups'), parts along dimension 0
There are 2 independent parts, one for each index of `groups`. A program takes and returns all parts, laid end to end along the dimension named above; an argument that names none is the same for every part. Nothing has to cross between parts.
Inputs may be any that keep to these rules, and one draw needn't show every extreme that they name: `head_kind`: exactly 4 of the 8 entries are 1, the others 0. `cache_len`: in every draw some request has all 32768 positions filled. `sink_len`: in every draw some request holds 128 sink tokens. `window_len`: in every draw some request holds 1920 recent tokens.
All inputs are finite; a program needn't handle non-finite values.
Results may differ from a plain program's by a relative error of at most 0.0075.
The roundings to bfloat16 on the way count: a program that leaves them out, or rounds other values in their place, can miss the bound.
Values may be sent and summed in bfloat16 or wider, within the bound.
No kernel may reach another device: no remote copies, remote signals or barrier semaphores. Data moves between devices by JAX's collectives and lax.ppermute only.
A program may use at most 128 MiB of HBM per device.

v0:
```python
import jax
import jax.numpy as jnp
from jax import lax
from jax.sharding import PartitionSpec as P

SINK_CAP = 128
epsilon = 1e-05
floor_score = -1e30


def joined(part, axis, combine):
    gathered = jax.tree.map(lambda a: lax.all_gather(a, axis), part)

    def take(source):
        return jax.tree.map(lambda a: lax.dynamic_index_in_dim(a, source, 0, False), gathered)

    return lax.fori_loop(
        1, lax.axis_size(axis), lambda source, state: combine(state, take(source)), take(0)
    )


def block_stats(queries, cache_keys, cache_values, visible, score_scale):
    scores = (
        jnp.einsum("bhqd,bhld->bhql", queries, cache_keys, preferred_element_type=jnp.float32)
        * score_scale
    )
    scores = jnp.where(visible, scores, floor_score)
    peak_score = jnp.max(scores, axis=-1)
    weights = jnp.where(visible, jnp.exp(scores - peak_score[..., None]), 0.0)
    weight_total = jnp.sum(weights, axis=-1)
    block_out = jnp.einsum(
        "bhql,bhld->bhqd",
        weights.astype(jnp.bfloat16),
        cache_values,
        preferred_element_type=jnp.float32,
    )
    return (peak_score, weight_total, block_out)


def spread_rows(values_in, selector):
    return jnp.einsum("brq,gr->bgq", values_in, selector, precision=lax.Precision.HIGHEST)


def spread_vectors(values_in, selector):
    return jnp.einsum("brqd,gr->bgqd", values_in, selector, precision=lax.Precision.HIGHEST)


def join_parts(first_part, second_part):
    top_score = jnp.maximum(first_part[0], second_part[0])
    left_factor = jnp.exp(first_part[0] - top_score)
    right_factor = jnp.exp(second_part[0] - top_score)
    joined_total = first_part[1] * left_factor + second_part[1] * right_factor
    joined_out = first_part[2] * left_factor[..., None] + second_part[2] * right_factor[..., None]
    return (top_score, joined_total, joined_out)


def per_device(
    hidden,
    norm_gain,
    q_weight,
    kv_weight,
    out_weight,
    head_kind,
    ret_keys,
    ret_values,
    stream_keys,
    stream_values,
    cache_len,
    sink_len,
    window_len,
):
    requests, drafts, local_width = hidden.shape
    kv_heads = head_kind.shape[0]
    head_dim = ret_keys.shape[3]
    retrieval = ret_keys.shape[1]
    running = stream_keys.shape[1]
    head_count = q_weight.shape[1] // head_dim
    group_size = head_count // kv_heads
    query_rows = drafts * group_size
    devices = lax.axis_size("seq")
    position = lax.axis_index("seq")
    tokens = requests * drafts
    hidden32 = hidden.astype(jnp.float32)
    squares = lax.psum(jnp.sum(hidden32 * hidden32, axis=-1), "seq")
    inverse = lax.rsqrt(squares / (local_width * devices) + epsilon)
    normed = (hidden32 * inverse[..., None] * norm_gain.astype(jnp.float32)).astype(jnp.bfloat16)
    flat_rows = normed.reshape(tokens, local_width)
    part_query = jnp.dot(flat_rows, q_weight, preferred_element_type=jnp.float32)
    part_fresh = jnp.dot(flat_rows, kv_weight, preferred_element_type=jnp.float32)
    whole_query, whole_fresh = lax.psum((part_query, part_fresh), "seq")
    queries = whole_query.astype(jnp.bfloat16)
    new_entries = whole_fresh.astype(jnp.bfloat16)
    grouped = (
        queries.reshape(requests, drafts, kv_heads, group_size, head_dim)
        .transpose(0, 2, 1, 3, 4)
        .reshape(requests, kv_heads, query_rows, head_dim)
    )
    fresh_split = new_entries.reshape(requests, drafts, 2, kv_heads, head_dim)
    new_keys = fresh_split[:, :, 0].transpose(0, 2, 1, 3)
    new_values = fresh_split[:, :, 1].transpose(0, 2, 1, 3)
    kind_flag = head_kind == 1
    rank_ret = jnp.cumsum(head_kind) - 1
    rank_str = jnp.cumsum(1 - head_kind) - 1
    select_ret = (
        kind_flag[:, None] & (rank_ret[:, None] == jnp.arange(retrieval)[None, :])
    ).astype(jnp.float32)
    select_str = (
        jnp.logical_not(kind_flag)[:, None] & (rank_str[:, None] == jnp.arange(running)[None, :])
    ).astype(jnp.float32)
    ret_queries = jnp.einsum(
        "bgqd,gr->brqd",
        grouped,
        select_ret.astype(jnp.bfloat16),
        preferred_element_type=jnp.float32,
    ).astype(jnp.bfloat16)
    str_queries = jnp.einsum(
        "bgqd,gr->brqd",
        grouped,
        select_str.astype(jnp.bfloat16),
        preferred_element_type=jnp.float32,
    ).astype(jnp.bfloat16)
    score_scale = head_dim ** (-0.5)
    cache_block = ret_keys.shape[2]
    cache_pos = position * cache_block + jnp.arange(cache_block)
    ret_visible = (cache_pos[None, :] < cache_len[:, None])[:, None, None, :]
    slot_block = stream_keys.shape[2]
    slot_pos = (position * slot_block + jnp.arange(slot_block))[None, :]
    sink_part = slot_pos < sink_len[:, None]
    recent_part = (slot_pos >= SINK_CAP) & (slot_pos < SINK_CAP + window_len[:, None])
    str_visible = (sink_part | recent_part)[:, None, None, :]
    ret_peak, ret_total, ret_out = block_stats(
        ret_queries, ret_keys, ret_values, ret_visible, score_scale
    )
    str_peak, str_total, str_out = block_stats(
        str_queries, stream_keys, stream_values, str_visible, score_scale
    )
    peak_all = spread_rows(ret_peak, select_ret) + spread_rows(str_peak, select_str)
    total_all = spread_rows(ret_total, select_ret) + spread_rows(str_total, select_str)
    out_all = spread_vectors(ret_out, select_ret) + spread_vectors(str_out, select_str)
    token_of_row = jnp.arange(query_rows) // group_size
    new_visible = jnp.arange(drafts)[None, :] <= token_of_row[:, None]
    new_peak, new_total, new_out = block_stats(
        grouped, new_keys, new_values, new_visible, score_scale
    )
    own_width = out_weight.shape[0]
    cache_peak, cache_total, cache_out = joined((peak_all, total_all, out_all), "seq", join_parts)
    top_score = jnp.maximum(cache_peak, new_peak)
    cache_factor = jnp.exp(cache_peak - top_score)
    new_factor = jnp.exp(new_peak - top_score)
    denominator = cache_total * cache_factor + new_total * new_factor
    attended = (
        cache_out * cache_factor[..., None] + new_out * new_factor[..., None]
    ) / denominator[..., None]
    attention = (
        attended.reshape(requests, kv_heads, drafts, group_size, head_dim)
        .transpose(0, 2, 1, 3, 4)
        .reshape(tokens, head_count * head_dim)
        .astype(jnp.bfloat16)
    )
    own_attention = lax.dynamic_slice_in_dim(attention, position * own_width, own_width, 1)
    own_output = lax.psum_scatter(
        lax.dot_general(
            out_weight, own_attention, (((0,), (1,)), ((), ())), preferred_element_type=jnp.float32
        ),
        "seq",
        scatter_dimension=0,
        tiled=True,
    )
    layer_output = own_output.T.reshape(requests, drafts, local_width).astype(jnp.bfloat16)
    return (layer_output, new_entries.reshape(requests, drafts, 2 * kv_heads * head_dim))


def solution(mesh):
    in_specs = (
        P("groups", None, "seq"),
        P("seq"),
        P("seq", None),
        P("seq", None),
        P("seq", None),
        P(),
        P("groups", None, "seq", None),
        P("groups", None, "seq", None),
        P("groups", None, "seq", None),
        P("groups", None, "seq", None),
        P("groups"),
        P("groups"),
        P("groups"),
    )
    out_specs = (P("groups", None, "seq"), P("groups", None, None))
    return jax.shard_map(
        per_device, mesh=mesh, in_specs=in_specs, out_specs=out_specs, check_vma=False
    )
```

profile of v0, /device:TPU:0, one launch (start us, length us, event | category | flops | bytes accessed | tf_op | source)
XLA Modules:
  0.0 258.6 jit_solution(16587945270876655756)
XLA Ops:
  7.3 0.8 subtract_bitcast_fusion
  9.4 0.8 reduce-window.16
  10.4 0.8 fusion.37
  11.2 34.9 %psum.21 = f32[2,4]{1,0:T(2,128)S(1)} all-reduce(f32[2,4]{1,0:T(2,128)S(1)} %fusion.37), channel_id=1, replica_groups=mesh['groups'=2,'seq'=16] {'seq'}, use_global_device_ids=true, to_apply=%region_2.0 | all-reduce | flops 8 | bytes 64 | tf_op jit(solution)/shard_map/psum | solution.py:84
  46.8 0.8 fusion.39
  48.0 4.6 %fusion.73 = f32[8,8192]{1,0:T(8,128)S(1)} fusion(bf16[8,512]{1,0:T(8,128)(2,1)S(1)} %reshape.194, bf16[512,8192]{1,0:T(8,128)(2,1)} %param.17), kind=kOutput, calls=%fused_computation.113 | convolution fusion | flops 67108864 | bytes 8658944 | tf_op jit(solution)/shard_map/dot_general | solution.py:88
  52.6 60.7 %all-reduce.2 = (bf16[8,8192]{1,0:T(8,128)(2,1)S(1)}, bf16[8,2048]{1,0:T(8,128)(2,1)S(1)}) all-reduce(f32[8,8192]{1,0:T(8,128)S(1)} %fusion.73, f32[8,2048]{1,0:T(8,128)S(1)} %fusion.74), channel_id=1, replica_groups=mesh['groups'=2,'seq'=16] {'seq'}, use_global_device_ids=true, to_apply=%region_3.0 | all-reduce | flops 81920 | bytes 491520 | tf_op jit(solution)/shard_map/psum | solution.py:90
  113.7 3.9 %fusion.70 = (f32[2,4,32]{2,1,0:T(4,128)S(1)}, f32[2,4,32,2048]{3,2,1,0:T(8,128)S(1)}) fusion(bf16[2,4,2048,128]{3,2,1,0:T(8,128)(2,1)} %param.21, bf16[2,4,32,128]{3,1,2,0:T(4,128)(2,1)S(1)} %fusion.12, pred[2,2048]{1,0:T(4,128)(4,1)S(1)} %broadcast_compare_fusion), kind=kOutput, calls=%fused_computation.110 | convolution fusion | flops 135790336 | bytes 6362112 | tf_op jit(solution)/shard_map/bhqd,bhld->bhql/dot_general | solution.py:24
  117.7 0.9 fusion.17
  121.5 2.1 fusion.5
  124.0 17.6 %all-gather.1 = f32[32,8,32]{2,1,0:T(8,128)S(1)} all-gather(f32[2,8,32]{2,1,0:T(8,128)S(1)} %fusion.15), channel_id=3, replica_groups=mesh['groups'=2,'seq'=16] {'seq'}, dimensions={0}, use_global_device_ids=true | all-gather | bytes 34816 | tf_op jit(solution)/shard_map/all_gather | solution.py:12
  142.0 20.1 %all-gather = f32[32,8,32]{2,1,0:T(8,128)S(1)} all-gather(f32[2,8,32]{2,1,0:T(8,128)S(1)} %fusion.16), channel_id=2, replica_groups=mesh['groups'=2,'seq'=16] {'seq'}, dimensions={0}, use_global_device_ids=true | all-gather | bytes 34816 | tf_op jit(solution)/shard_map/all_gather | solution.py:12
  162.4 7.8 %all-gather.5.cloned.1.call-done = f32[32,8,32,128]{3,2,1,0:T(8,128)} async-done(((f32[2,8,32,128]{3,2,1,0:T(8,128)}), f32[32,8,32,128]{3,2,1,0:T(8,128)}) %all-gather.5.cloned.1.call-update) | async-done | bytes 4194320 | tf_op jit(solution)/shard_map/all_gather | solution.py:12
  170.2 1.0 slice.16
  171.2 18.9 %while.19 = (s32[]{:T(128)}, f32[2,8,32]{2,1,0:T(8,128)S(1)}, f32[2,8,32]{2,1,0:T(8,128)S(1)}, f32[2,8,32,128]{3,2,1,0:T(8,128)S(1)}, f32[16,2,8,32]{3,2,1,0:T(8...) while((s32[]{:T(128)}, f32[2,8,32]{2,1,0:T(8,128)S(1)}, ...), condition=%wide.region_10.11_spmd, body=%wide.region_9.10_spmd.sunk | while | flops 199685 | bytes 807055 | solution.py:17
  171.2 1.2 fusion.93
  172.5 1.2 fusion.93
  173.7 1.2 fusion.93
  175.0 1.2 fusion.93
  176.3 1.2 fusion.93
  177.5 1.2 fusion.93
  178.8 1.2 fusion.93
  180.1 1.2 fusion.93
  181.3 1.2 fusion.93
  182.6 1.2 fusion.93
  183.8 1.2 fusion.93
  185.1 1.2 fusion.93
  186.4 1.2 fusion.93
  187.6 1.2 fusion.93
  188.9 1.2 fusion.93
  190.6 5.3 %convolution_bitcast_fusion = f32[8192,8]{0,1:T(8,128)} fusion(bf16[512,8192]{1,0:T(8,128)(2,1)} %param.19, bf16[8,8192]{1,0:T(8,128)(2,1)S(1)} %convert_element_type.88, s32[]{:T(128)S(6)} %select_n.59), kind=kOutput, calls=%fused_computation.8 | convolution fusion | flops 67108864 | bytes 8658948 | tf_op jit(solution)/shard_map/dot_general | solution.py:162
  196.6 53.8 %reduce-scatter.2.cloned.1.call-done = f32[512,8]{0,1:T(8,128)} async-done(((f32[8192,8]{0,1:T(8,128)}), f32[512,8]{0,1:T(8,128)}) %reduce-scatter.2.cloned.1.call-update) | async-done | bytes 16400 | tf_op jit(solution)/shard_map/reduce_scatter | solution.py:161
  (77 shorter events, 9.7 us)
Async XLA Ops:
  7.2 40.4 %copy-start = (bf16[512,2048]{1,0:T(8,128)(2,1)S(1)}, bf16[512,2048]{1,0:T(8,128)(2,1)}, u32[]{:S(2)}) copy-start(bf16[512,2048]{1,0:T(8,128)(2,1)} %param.18) | copy-start | bytes 6291460
  7.2 163.0 %all-gather.5.cloned.1.call-start = ((), (), s32[]{:S(2)}) async-start(), calls=%async_computation.2 | async-start | bytes 4456448 | tf_op jit(solution)/shard_map/all_gather | solution.py:12
  48.0 65.7 %copy-start.5 = (s32[2]{0:T(128)S(1)}, s32[2]{0:T(128)}, u32[]{:S(2)}) copy-start(s32[2]{0:T(128)} %param.25) | copy-start | bytes 28
  113.7 4.0 %copy-start.2 = (bf16[2,4,2048,128]{3,2,1,0:T(8,128)(2,1)S(1)}, bf16[2,4,2048,128]{3,2,1,0:T(8,128)(2,1)}, u32[]{:S(2)}) copy-start(bf16[2,4,2048,128]{3,2,1,0:T(8,128)(2,1)} %param.22) | copy-start | bytes 12582916
  117.7 1.3 copy-start.1
  117.7 1.7 copy-start.6
  117.7 1.8 copy-start.4
  117.7 2.1 copy-start.3
  121.2 129.2 %reduce-scatter.2.cloned.1.call-start = ((), (), s32[]{:S(2)}) async-start(), calls=%async_computation.1 | async-start | bytes 278528 | tf_op jit(solution)/shard_map/reduce_scatter | solution.py:161
Sparse Core Ops, SparseCore 0:
  121.3 48.8 all-gather.4
  196.0 54.3 reduce-scatter.1
where the time goes:
time: 260 us; the launch traced here: 259 us
  blocking collectives  133 us (51%)
  waiting for transfers between devices  61.7 us (24%)
  other arithmetic  27.2 us (10%)
  matrix products  18 us (7%)
  between operations  14.3 us (6%)
  local copies, waits for them, and re-layouts  3.58 us (1%)
    psum x1, blocking collectives, per_device(): whole_query, whole_fresh = lax.psum((part_query, part_fresh), 'seq')  60.7 us
    reduce_scatter x1, waiting for transfers between devices, per_device(): lax.psum_scatter(lax.dot_general(out_weight, own_attention, (((0,), (1,))...  53.8 us
    all_gather x2, blocking collectives, joined(): gathered = jax.tree.map(lambda a: lax.all_gather(a, axis), part)  37.7 us
    psum x1, blocking collectives, per_device(): squares = lax.psum(jnp.sum(hidden32 * hidden32, axis=-1), 'seq')  34.9 us
    add x15, other arithmetic, join_parts(): first_part[2] * left_factor[..., None]  18.2 us
    all_gather x1, waiting for transfers between devices, joined(): gathered = jax.tree.map(lambda a: lax.all_gather(a, axis), part)  7.8 us
    dot_general x1, matrix products, per_device(): lax.dot_general(out_weight, own_attention, (((0,), (1,)), ((), ())), pref...  5.28 us
  transfers between devices with their start and end apart: 2, of which 2 were waited for; matrix products, arithmetic and copies ran while one was open for 2% of the time, Pallas kernels for 0%

commit v1 on v0

--- a/solution.py
+++ b/solution.py
@@ -81,7 +81,7 @@
     position = lax.axis_index("seq")
     tokens = requests * drafts
     hidden32 = hidden.astype(jnp.float32)
-    squares = lax.psum(jnp.sum(hidden32 * hidden32, axis=-1), "seq")
+    squares = jnp.sum(lax.all_gather(jnp.sum(hidden32 * hidden32, axis=-1), "seq"), axis=0)
     inverse = lax.rsqrt(squares / (local_width * devices) + epsilon)
     normed = (hidden32 * inverse[..., None] * norm_gain.astype(jnp.float32)).astype(jnp.bfloat16)
     flat_rows = normed.reshape(tokens, local_width)

time: 260 us -> 248 us (0.954)
  blocking collectives: 133 us -> 122 us
    psum x1 -> x0, blocking collectives: 34.9 us -> none  [per_device(): squares = lax.psum(jnp.sum(hidden32 * hidden32, axis=-1), 'seq')]
    all_gather x0 -> x1, blocking collectives: none -> 23.1 us  [per_device(): lax.all_gather(jnp.sum(hidden32 * hidden32, axis=-1), 'seq')]
where the time goes in v1:
time: 248 us; the launch traced here: 247 us
  blocking collectives  122 us (49%)
  waiting for transfers between devices  61.7 us (25%)
  other arithmetic  27.2 us (11%)
  matrix products  18 us (7%)
  between operations  14.3 us (6%)
  local copies, waits for them, and re-layouts  3.58 us (1%)
    psum x1, blocking collectives, per_device(): whole_query, whole_fresh = lax.psum((part_query, part_fresh), 'seq')  61 us
    reduce_scatter x1, waiting for transfers between devices, per_device(): lax.psum_scatter(lax.dot_general(out_weight, own_attention, (((0,), (1,))...  53.8 us
    all_gather x2, blocking collectives, joined(): gathered = jax.tree.map(lambda a: lax.all_gather(a, axis), part)  37.7 us
    all_gather x1, blocking collectives, per_device(): lax.all_gather(jnp.sum(hidden32 * hidden32, axis=-1), 'seq')  23.1 us
    add x15, other arithmetic, join_parts(): first_part[2] * left_factor[..., None]  18.2 us
    all_gather x1, waiting for transfers between devices, joined(): gathered = jax.tree.map(lambda a: lax.all_gather(a, axis), part)  7.8 us
    dot_general x1, matrix products, per_device(): lax.dot_general(out_weight, own_attention, (((0,), (1,)), ((), ())), pref...  5.28 us
  transfers between devices with their start and end apart: 2, of which 2 were waited for; matrix products, arithmetic and copies ran while one was open for 2% of the time, Pallas kernels for 0%

profile of v1, /device:TPU:0, one launch (start us, length us, event | category | flops | bytes accessed | tf_op | source)
XLA Modules:
  0.0 247.1 jit_solution(14069878124488916538)
XLA Ops:
  7.3 0.8 subtract_bitcast_fusion
  9.4 0.8 reduce-window.16
  10.4 0.8 fusion.37
  11.9 23.1 %all-gather.4 = f32[16,2,4]{2,1,0:T(2,128)S(1)} all-gather(f32[1,2,4]{2,1,0:T(2,128)S(1)} %bitcast.130), channel_id=2, replica_groups=mesh['groups'=2,'seq'=16] {'seq'}, dimensions={0}, use_global_device_ids=true | all-gather | bytes 544 | tf_op jit(solution)/shard_map/all_gather | solution.py:84
  35.0 0.8 fusion.39
  36.2 4.6 %fusion.73 = f32[8,8192]{1,0:T(8,128)S(1)} fusion(bf16[8,512]{1,0:T(8,128)(2,1)S(1)} %reshape.198, bf16[512,8192]{1,0:T(8,128)(2,1)} %param.17), kind=kOutput, calls=%fused_computation.113 | convolution fusion | flops 67108864 | bytes 8658944 | tf_op jit(solution)/shard_map/dot_general | solution.py:88
  40.8 61.0 %all-reduce.2 = (bf16[8,8192]{1,0:T(8,128)(2,1)S(1)}, bf16[8,2048]{1,0:T(8,128)(2,1)S(1)}) all-reduce(f32[8,8192]{1,0:T(8,128)S(1)} %fusion.73, f32[8,2048]{1,0:T(8,128)S(1)} %fusion.74), channel_id=1, replica_groups=mesh['groups'=2,'seq'=16] {'seq'}, use_global_device_ids=true, to_apply=%region_3.0 | all-reduce | flops 81920 | bytes 491520 | tf_op jit(solution)/shard_map/psum | solution.py:90
  102.3 3.9 %fusion.70 = (f32[2,4,32]{2,1,0:T(4,128)S(1)}, f32[2,4,32,2048]{3,2,1,0:T(8,128)S(1)}) fusion(bf16[2,4,2048,128]{3,2,1,0:T(8,128)(2,1)} %param.21, bf16[2,4,32,128]{3,1,2,0:T(4,128)(2,1)S(1)} %fusion.12, pred[2,2048]{1,0:T(4,128)(4,1)S(1)} %broadcast_compare_fusion), kind=kOutput, calls=%fused_computation.110 | convolution fusion | flops 135790336 | bytes 6362112 | tf_op jit(solution)/shard_map/bhqd,bhld->bhql/dot_general | solution.py:24
  106.3 0.9 fusion.17
  110.0 2.1 fusion.5
  112.5 17.6 %all-gather.2 = f32[32,8,32]{2,1,0:T(8,128)S(1)} all-gather(f32[2,8,32]{2,1,0:T(8,128)S(1)} %fusion.15), channel_id=4, replica_groups=mesh['groups'=2,'seq'=16] {'seq'}, dimensions={0}, use_global_device_ids=true | all-gather | bytes 34816 | tf_op jit(solution)/shard_map/all_gather | solution.py:12
  130.5 20.1 %all-gather.1 = f32[32,8,32]{2,1,0:T(8,128)S(1)} all-gather(f32[2,8,32]{2,1,0:T(8,128)S(1)} %fusion.16), channel_id=3, replica_groups=mesh['groups'=2,'seq'=16] {'seq'}, dimensions={0}, use_global_device_ids=true | all-gather | bytes 34816 | tf_op jit(solution)/shard_map/all_gather | solution.py:12
  150.9 7.8 %all-gather.7.cloned.1.call-done = f32[32,8,32,128]{3,2,1,0:T(8,128)} async-done(((f32[2,8,32,128]{3,2,1,0:T(8,128)}), f32[32,8,32,128]{3,2,1,0:T(8,128)}) %all-gather.7.cloned.1.call-update) | async-done | bytes 4194320 | tf_op jit(solution)/shard_map/all_gather | solution.py:12
  158.7 1.0 slice.16
  159.7 19.0 %while.19 = (s32[]{:T(128)}, f32[2,8,32]{2,1,0:T(8,128)S(1)}, f32[2,8,32]{2,1,0:T(8,128)S(1)}, f32[2,8,32,128]{3,2,1,0:T(8,128)S(1)}, f32[16,2,8,32]{3,2,1,0:T(8...) while((s32[]{:T(128)}, f32[2,8,32]{2,1,0:T(8,128)S(1)}, ...), condition=%wide.region_10.11_spmd, body=%wide.region_9.10_spmd.sunk | while | flops 199685 | bytes 807055 | solution.py:17
  159.8 1.2 fusion.93
  161.0 1.2 fusion.93
  162.3 1.2 fusion.93
  163.6 1.2 fusion.93
  164.8 1.2 fusion.93
  166.1 1.2 fusion.93
  167.3 1.2 fusion.93
  168.6 1.2 fusion.93
  169.9 1.2 fusion.93
  171.1 1.2 fusion.93
  172.4 1.2 fusion.93
  173.7 1.2 fusion.93
  174.9 1.2 fusion.93
  176.2 1.2 fusion.93
  177.5 1.2 fusion.93
  179.2 5.3 %convolution_bitcast_fusion = f32[8192,8]{0,1:T(8,128)} fusion(bf16[512,8192]{1,0:T(8,128)(2,1)} %param.19, bf16[8,8192]{1,0:T(8,128)(2,1)S(1)} %convert_element_type.88, s32[]{:T(128)S(6)} %select_n.59), kind=kOutput, calls=%fused_computation.8 | convolution fusion | flops 67108864 | bytes 8658948 | tf_op jit(solution)/shard_map/dot_general | solution.py:162
  185.1 53.8 %reduce-scatter.2.cloned.1.call-done = f32[512,8]{0,1:T(8,128)} async-done(((f32[8192,8]{0,1:T(8,128)}), f32[512,8]{0,1:T(8,128)}) %reduce-scatter.2.cloned.1.call-update) | async-done | bytes 16400 | tf_op jit(solution)/shard_map/reduce_scatter | solution.py:161
  (78 shorter events, 9.8 us)
Async XLA Ops:
  7.2 28.6 %copy-start = (bf16[512,2048]{1,0:T(8,128)(2,1)S(1)}, bf16[512,2048]{1,0:T(8,128)(2,1)}, u32[]{:S(2)}) copy-start(bf16[512,2048]{1,0:T(8,128)(2,1)} %param.18) | copy-start | bytes 6291460
  7.2 151.6 %all-gather.7.cloned.1.call-start = ((), (), s32[]{:S(2)}) async-start(), calls=%async_computation.2 | async-start | bytes 4456448 | tf_op jit(solution)/shard_map/all_gather | solution.py:12
  36.2 66.0 %copy-start.5 = (s32[2]{0:T(128)S(1)}, s32[2]{0:T(128)}, u32[]{:S(2)}) copy-start(s32[2]{0:T(128)} %param.25) | copy-start | bytes 28
  102.3 4.0 %copy-start.2 = (bf16[2,4,2048,128]{3,2,1,0:T(8,128)(2,1)S(1)}, bf16[2,4,2048,128]{3,2,1,0:T(8,128)(2,1)}, u32[]{:S(2)}) copy-start(bf16[2,4,2048,128]{3,2,1,0:T(8,128)(2,1)} %param.22) | copy-start | bytes 12582916
  106.2 1.3 copy-start.1
  106.2 1.7 copy-start.6
  106.3 1.8 copy-start.4
  106.3 2.1 copy-start.3
  109.8 129.2 %reduce-scatter.2.cloned.1.call-start = ((), (), s32[]{:S(2)}) async-start(), calls=%async_computation.1 | async-start | bytes 278528 | tf_op jit(solution)/shard_map/reduce_scatter | solution.py:161
Sparse Core Ops, SparseCore 0:
  109.9 48.8 all-gather.6
  184.6 54.2 reduce-scatter.1
